TPU v7x, 128 devices: a whole 4x4x4 slice. The times are simulated.
128 devices in a mesh: batch: 4 (over z_hi, core), centers: 32 (over x, y, z_lo).
Axes of the slice: x: 4, y: 4, z: 4 (z_hi: 2, z_lo: 2; z = z_hi * 2 + z_lo), core: 2. Of those that a mesh axis runs over, the one named last changes fastest.
Arguments:
- pool_features: float32 [131072, 128], P(('batch', 'centers')), may hold values from -14 to 14
- pool_targets: float32 [131072, 64], P(('batch', 'centers')), may hold values from -6 to 6
- batch_index: int32 [8192], P(('batch', 'centers')), may hold values from 0 to 1023
- centers: float32 [16384, 128], P('centers'), may hold values from -14 to 14
- weights: float32 [16384, 64], P('centers'), as said below
- eig_vectors: float32 [16384, 1024], P(('batch', 'centers')), may hold values from -0.046875 to 0.046875
- eig_scale: float32 [1024], replicated, may hold values from 0.5 to 4
- nys_owner: int32 [16384, 1], P(('batch', 'centers')), may hold values from 0 to 31; in each aligned block of 128 rows (0 to 127, 128 to 255, ...) at most 8 rows name the same one
- nys_offset: int32 [16384], P(('batch', 'centers')), may hold values from 0 to 511
Outputs:
- residual_out: float32 [8192, 64], P(('batch', 'centers'))
- update: float32 [16384, 64], P('centers')
Inputs may be any that keep to these rules, and one draw needn't show every extreme that they name: `nys_owner`: among the 128 rows of one device no owner is named more than 8 times; on some devices one owner is named exactly 8 times. `weights`: every column sums to zero.
All inputs are finite; a program needn't handle non-finite values.
Results may differ from a plain program's by a relative error of at most 0.0003.
Values sent between devices are 32-bit elements; how exact they have to be, the bound alone decides.
No kernel may reach another device: no remote copies, remote signals or barrier semaphores. Data moves between devices by JAX's collectives and lax.ppermute only.
A program may use at most 64 MiB of HBM per device.

v0:
```python
import math
import jax
import jax.numpy as jnp
from jax import lax
from jax.sharding import PartitionSpec as P

DEPTH = 3
epsilon = 1e-06
highest = lax.Precision.HIGHEST


def kernel_rows(row_block, center_block, center_norm):
    inner_prod = (
        lax.dot_general(
            row_block,
            center_block,
            (((1,), (1,)), ((), ())),
            precision=highest,
            preferred_element_type=jnp.float32,
        )
        / row_block.shape[1]
    )
    row_norm = jnp.mean(row_block * row_block, axis=1) + epsilon
    norm_scale = jnp.sqrt(row_norm[:, None] * center_norm[None, :])
    sigma_now = inner_prod
    tangent = inner_prod
    for depth_step in range(DEPTH):
        cosine = sigma_now / norm_scale
        arc_angle = jnp.arccos(cosine)
        remain = (math.pi - arc_angle) / math.pi
        sigma_now = (
            norm_scale
            * (jnp.sqrt(1.0 - cosine * cosine) + (math.pi - arc_angle) * cosine)
            / math.pi
        )
        tangent = sigma_now + tangent * remain
    return tangent


def per_device(
    pool_features,
    pool_targets,
    batch_index,
    centers,
    weights,
    eig_vectors,
    eig_scale,
    nys_owner,
    nys_offset,
):
    local_rows = pool_features[batch_index]
    local_targets = pool_targets[batch_index]
    row_count = local_rows.shape[0]
    group_size = lax.axis_size("centers")
    rows_total = row_count * group_size * lax.axis_size("batch")
    center_count = centers.shape[0]
    outputs = weights.shape[1]
    center_norm = jnp.mean(centers * centers, axis=1) + epsilon
    kernel = kernel_rows(
        lax.all_gather(local_rows, "centers", axis=0, tiled=True), centers, center_norm
    )
    partial_pred = jnp.dot(kernel, weights, precision=highest, preferred_element_type=jnp.float32)
    all_targets = lax.all_gather(local_targets, "centers", axis=0, tiled=True)
    prediction = lax.psum(partial_pred, "centers")
    residual = prediction - all_targets
    own_residual = lax.dynamic_slice_in_dim(
        residual, lax.axis_index("centers") * row_count, row_count, 0
    )
    grads_part = lax.dot_general(
        kernel,
        residual,
        (((0,), (0,)), ((), ())),
        precision=highest,
        preferred_element_type=jnp.float32,
    ) / math.sqrt(rows_total)
    grads = lax.psum(grads_part, "batch")
    owner = nys_owner[:, 0]
    slots = max(2, 2 * owner.shape[0] // group_size)
    owner_hot = (owner[:, None] == jnp.arange(group_size, dtype=jnp.int32)[None, :]).astype(
        jnp.int32
    )
    slot_rank = jnp.sum((jnp.cumsum(owner_hot, axis=0) - owner_hot) * owner_hot, axis=1)
    requests = jnp.zeros((group_size, slots), jnp.int32).at[owner, slot_rank].set(nys_offset)
    received = lax.all_to_all(requests, "centers", split_axis=0, concat_axis=0, tiled=True)
    found = grads[received]
    returned = lax.all_to_all(found, "centers", split_axis=0, concat_axis=0, tiled=True)
    picked_grads = returned[owner, slot_rank]
    coeff_part = lax.dot_general(
        eig_vectors,
        picked_grads,
        (((0,), (0,)), ((), ())),
        precision=highest,
        preferred_element_type=jnp.float32,
    )
    coeff = lax.psum(coeff_part, ("batch", "centers"))
    corr_rows = jnp.dot(
        eig_vectors,
        eig_scale[:, None] * coeff,
        precision=highest,
        preferred_element_type=jnp.float32,
    )
    spread = (
        jnp.zeros((group_size * center_count, outputs), jnp.float32)
        .at[owner * center_count + nys_offset]
        .add(corr_rows)
    )
    corr_part = lax.psum_scatter(spread, "centers", scatter_dimension=0, tiled=True)
    correction = lax.psum(corr_part, "batch")
    return (own_residual, correction - grads)


def solution(mesh):
    placed = (
        P(("batch", "centers"), None),
        P(("batch", "centers"), None),
        P(("batch", "centers")),
        P("centers", None),
        P("centers", None),
        P(("batch", "centers"), None),
        P(),
        P(("batch", "centers"), None),
        P(("batch", "centers")),
    )
    return jax.shard_map(
        per_device,
        mesh=mesh,
        in_specs=placed,
        out_specs=(P(("batch", "centers"), None), P("centers", None)),
        check_vma=False,
    )
```

profile of v0, /device:TPU:1, one launch (start us, length us, event | category | flops | bytes accessed | tf_op | source)
XLA Modules:
  0.0 951.3 jit_solution(6418293287864881805)
XLA Ops:
  7.2 0.0 copy-start
  7.2 0.0 all-gather.4.cloned.1.call-start
  7.2 0.7 compare_select_fusion.4
  7.9 2.2 gather_fusion
  10.2 0.0 all-gather.4.cloned.1.call-update
  10.2 0.0 all-reduce.5.cloned.1.call-start
  10.2 0.7 fusion.4
  11.0 0.2 reduce_window_sum.11
  11.2 1.1 multiply_reduce_fusion.1
  12.3 130.2 %all-gather.4.cloned.1.call-done = f32[2048,128]{1,0:T(8,128)} async-done(((f32[64,128]{1,0:T(8,128)}), f32[2048,128]{1,0:T(8,128)}) %all-gather.4.cloned.1.call-update) | async-done | bytes 1048592 | tf_op jit(solution)/shard_map/all_gather | solution.py:60
  142.5 1.6 multiply_reduce_fusion
  144.1 0.0 copy-start.4
  144.1 37.0 %multiply_add_fusion = f32[2048,512]{1,0:T(8,128)S(1)} fusion(f32[2048,128]{1,0:T(8,128)} %all-gather.4.cloned.1.call-done, f32[512,128]{1,0:T(8,128)} %param.12, f32[512]{0:T(512)S(1)} %multiply_add_fusion.2, f32[2048]{0:T(1024)S(1)} %multiply_add_fusion.1), kind=kOutput, calls=%fused_computation.8 | convolution fusion | flops 1656750080 | bytes 5515264 | tf_op jit(solution)/shard_map/dot_general | solution.py:14
  181.0 0.0 copy-start.1
  181.1 1.9 copy-done.1
  183.0 0.0 copy-done.4
  183.0 5.0 fusion.8
  188.0 0.0 all-reduce.5.cloned.1.call-update
  188.0 0.0 copy-done.5
  188.0 0.2 select_reduce_fusion
  188.2 0.0 copy-done.7
  188.2 6.4 scatter_fusion
  194.7 0.7 copy.26
  195.4 6.9 all-to-all-start
  202.3 0.0 all-reduce.7.cloned.1.call-start
  202.4 0.0 copy-done.3
  202.4 0.2 copy.24
  202.6 0.6 gather_fusion.1
  203.2 73.5 %all-gather.1 = f32[2048,64]{1,0:T(8,128)S(1)} all-gather(f32[64,64]{1,0:T(8,128)S(1)} %gather_fusion.1), channel_id=3, replica_groups=mesh['batch'=4,'centers'=32] {'centers'}, dimensions={0}, use_global_device_ids=true | all-gather | bytes 540672 | tf_op jit(solution)/shard_map/all_gather | solution.py:63
  276.7 0.3 copy.25
  277.0 218.7 %all-reduce.5.cloned.1.call-done = f32[2048,64]{0,1:T(8,128)} async-done(((f32[2048,64]{0,1:T(8,128)}), f32[2048,64]{0,1:T(8,128)}) %all-reduce.5.cloned.1.call-update) | async-done | bytes 524304 | tf_op jit(solution)/shard_map/psum | solution.py:64
  495.7 1.1 sub.36
  496.9 5.6 convolution_multiply_fusion
  502.5 0.0 all-reduce.7.cloned.1.call-update
  502.5 0.0 all-reduce.9.cloned.1.call-start
  502.5 0.0 all-to-all-done
  502.6 0.1 reshape.74
  502.7 62.1 %all-reduce.7.cloned.1.call-done = f32[512,64]{0,1:T(8,128)} async-done(((f32[512,64]{0,1:T(8,128)}), f32[512,64]{0,1:T(8,128)}) %all-reduce.7.cloned.1.call-update) | async-done | bytes 131088 | tf_op jit(solution)/shard_map/psum | solution.py:76
  564.8 1.0 copy.27
  565.8 0.7 gather_fusion.2
  566.6 0.1 reshape.108
  566.7 13.8 %all_to_all.17 = f32[32,1,512]{2,1,0:T(1,128)S(1)} all-to-all(f32[32,1,512]{2,1,0:T(1,128)S(1)} %reshape.108), channel_id=1, replica_groups=mesh['batch'=4,'centers'=32] {'centers'}, dimensions={0} | all-to-all | bytes 131072 | tf_op jit(solution)/shard_map/all_to_all | solution.py:86
  580.5 0.5 broadcast.183
  581.0 0.8 reduce
  581.8 0.1 reshape.109
  581.9 1.0 gather_fusion.3
  582.9 0.0 copy-done
  582.9 1.1 convolution_bitcast_fusion
  584.0 0.0 all-reduce.9.cloned.1.call-update
  584.1 0.0 reduce-scatter.2.cloned.1.call-start
  584.1 139.3 %all-reduce.9.cloned.1.call-done = f32[1024,64]{0,1:T(8,128)} async-done(((f32[1024,64]{0,1:T(8,128)}), f32[1024,64]{0,1:T(8,128)}) %all-reduce.9.cloned.1.call-update) | async-done | bytes 262160 | tf_op jit(solution)/shard_map/psum | solution.py:95
  723.5 1.6 convolution_bitcast_fusion.1
  725.1 0.1 copy.28
  725.2 4.7 scatter_custom_fusion.1
  729.9 6.8 copy.29
  736.7 0.0 reduce-scatter.2.cloned.1.call-update
  736.7 0.0 all-reduce.11.cloned.1.call-start
  736.8 143.0 %reduce-scatter.2.cloned.1.call-done = f32[512,64]{0,1:T(8,128)} async-done(((f32[16384,64]{0,1:T(8,128)}), f32[512,64]{0,1:T(8,128)}) %reduce-scatter.2.cloned.1.call-update) | async-done | bytes 131088 | tf_op jit(solution)/shard_map/reduce_scatter | solution.py:107
  879.8 0.0 all-reduce.11.cloned.1.call-update
  879.8 0.1 constant_dynamic-slice_fusion
  879.9 0.7 copy.30
  880.6 62.3 %all-reduce.11.cloned.1.call-done = f32[512,64]{0,1:T(8,128)} async-done(((f32[512,64]{0,1:T(8,128)}), f32[512,64]{0,1:T(8,128)}) %all-reduce.11.cloned.1.call-update) | async-done | bytes 131088 | tf_op jit(solution)/shard_map/psum | solution.py:108
  942.8 0.0 copy-done.2
  942.9 1.6 sub.38
  (14 shorter events, 0.1 us)
Async XLA Ops:
  7.2 575.7 %copy-start = (f32[128,1024]{1,0:T(8,128)S(1)}, f32[128,1024]{1,0:T(8,128)}, u32[]{:S(2)}) copy-start(f32[128,1024]{1,0:T(8,128)} %param.14) | copy-start | bytes 1572868
  7.2 135.3 %all-gather.4.cloned.1.call-start = ((), (), s32[]{:S(2)}) async-start(), calls=%async_computation.8 | async-start | bytes 1081344 | tf_op jit(solution)/shard_map/all_gather | solution.py:60
  10.2 485.5 %all-reduce.5.cloned.1.call-start = ((), (), s32[]{:S(2)}) async-start(), calls=%async_computation.3 | async-start | bytes 1048576 | tf_op jit(solution)/shard_map/psum | solution.py:64
  144.1 38.9 %copy-start.4 = (f32[512,64]{0,1:T(8,128)S(1)}, f32[512,64]{0,1:T(8,128)}, u32[]{:S(2)}) copy-start(f32[512,64]{0,1:T(8,128)} %param.13) | copy-start | bytes 393220
  181.0 1.9 copy-start.1
  183.0 5.0 copy-start.5
  183.0 5.3 copy-start.7
  183.0 19.4 %copy-start.3 = (f32[1024,64]{0,1:T(8,128)S(1)}, f32[1024,64]{0,1:T(8,128)}, u32[]{:S(2)}) copy-start(f32[1024,64]{0,1:T(8,128)} %param.10) | copy-start | bytes 786436
  195.4 307.2 %all-to-all-start = ((s32[32,1,8]{2,1,0:T(1,128)}), s32[32,1,8]{2,1,0:T(1,128)S(1)}, u32[]{:S(2)}, u32[]{:S(2)}) async-start(s32[32,1,8]{2,1,0:T(1,128)} %copy.26), calls=%async_computation | async-start | bytes 32768 | tf_op jit(solution)/shard_map/all_to_all | solution.py:84
  202.3 362.5 %all-reduce.7.cloned.1.call-start = ((), (), s32[]{:S(2)}) async-start(), calls=%async_computation.4 | async-start | bytes 262144 | tf_op jit(solution)/shard_map/psum | solution.py:76
  496.9 226.6 %copy-start.6 = (f32[1024]{0:T(1024)S(1)}, f32[1024]{0:T(1024)}, u32[]{:S(2)}) copy-start(f32[1024]{0:T(1024)} %param.15) | copy-start | bytes 12292
  502.5 221.0 %all-reduce.9.cloned.1.call-start = ((), (), s32[]{:S(2)}) async-start(), calls=%async_computation.5 | async-start | bytes 524288 | tf_op jit(solution)/shard_map/psum | solution.py:95
  584.1 295.7 %reduce-scatter.2.cloned.1.call-start = ((), (), s32[]{:S(2)}) async-start(), calls=%async_computation.6 | async-start | bytes 4325376 | tf_op jit(solution)/shard_map/reduce_scatter | solution.py:107
  736.7 206.1 %copy-start.2 = (f32[512,64]{0,1:T(8,128)S(1)}, f32[512,64]{0,1:T(8,128)}, u32[]{:S(2)}) copy-start(f32[512,64]{0,1:T(8,128)} %all-reduce.7.cloned.1.call-done) | copy-start | bytes 393220
  736.7 206.1 %all-reduce.11.cloned.1.call-start = ((), (), s32[]{:S(2)}) async-start(), calls=%async_computation.7 | async-start | bytes 262144 | tf_op jit(solution)/shard_map/psum | solution.py:108
Sparse Core Ops, SparseCore 0:
  10.3 132.1 all-gather.3
  188.1 307.5 all-reduce.4
  502.6 62.1 all-reduce.6
  584.2 139.2 all-reduce.8
  736.9 142.8 reduce-scatter.1
  882.1 60.7 all-reduce.10
where the time goes:
time: 952 us; the launch traced here: 951 us
  waiting for transfers between devices  756 us (79%)
  blocking collectives  87.4 us (9%)
  matrix products  50.3 us (5%)
  local copies, waits for them, and re-layouts  23.6 us (2%)
  between operations  14.3 us (2%)
  other arithmetic  12.7 us (1%)
    psum x1, waiting for transfers between devices, per_device(): prediction = lax.psum(partial_pred, 'centers')  219 us
    reduce_scatter x1, waiting for transfers between devices, per_device(): lax.psum_scatter(spread, 'centers', scatter_dimension=0, tiled=True)  143 us
    psum x1, waiting for transfers between devices, per_device(): coeff = lax.psum(coeff_part, ('batch', 'centers'))  139 us
    all_gather x1, waiting for transfers between devices, per_device(): lax.all_gather(local_rows, 'centers', axis=0, tiled=True)  130 us
    all_gather x1, blocking collectives, per_device(): all_targets = lax.all_gather(local_targets, 'centers', axis=0, tiled=True)  73.5 us
    psum x1, waiting for transfers between devices, per_device(): correction = lax.psum(corr_part, 'batch')  62.3 us
    psum x1, waiting for transfers between devices, per_device(): grads = lax.psum(grads_part, 'batch')  62.1 us
    dot_general x1, matrix products, kernel_rows(): lax.dot_general(row_block, center_block, (((1,), (1,)), ((), ())), precis...  37 us
  transfers between devices with their start and end apart: 7, of which 6 were waited for; matrix products, arithmetic and copies ran while one was open for 2% of the time, Pallas kernels for 0%

commit v1 on v0

--- a/solution.py
+++ b/solution.py
@@ -61,7 +61,7 @@
     )
     partial_pred = jnp.dot(kernel, weights, precision=highest, preferred_element_type=jnp.float32)
     all_targets = lax.all_gather(local_targets, "centers", axis=0, tiled=True)
-    prediction = lax.psum(partial_pred, "centers")
+    prediction = jnp.sum(lax.all_gather(partial_pred, "centers"), axis=0)
     residual = prediction - all_targets
     own_residual = lax.dynamic_slice_in_dim(
         residual, lax.axis_index("centers") * row_count, row_count, 0

time: 952 us -> 1050 us (1.10)
  waiting for transfers between devices: 756 us -> 813 us
  local copies, waits for them, and re-layouts: 23.6 us -> 42.3 us
  blocking collectives: 87.4 us -> 104 us
    all_gather x0 -> x1, waiting for transfers between devices: none -> 296 us  [per_device(): prediction = jnp.sum(lax.all_gather(partial_pred, 'centers'), axis=0)]
    psum x1 -> x0, waiting for transfers between devices: 219 us -> none  [per_device(): prediction = lax.psum(partial_pred, 'centers')]
    psum x1, waiting for transfers between devices: 62.1 us -> 41.5 us  [per_device(): grads = lax.psum(grads_part, 'batch')]
    unnamed x20, local copies, waits for them, and re-layouts: 3.06 us -> 20.2 us
    all_gather x1, blocking collectives: 73.5 us -> 90.6 us  [per_device(): all_targets = lax.all_gather(local_targets, 'centers', axis=0, tiled=True)]
  transfers between devices with their start and end apart: 7 -> 7, of which waited for: 6 -> 6; matrix products, arithmetic and copies ran while one was open for 2% -> 4% of each run, Pallas kernels for 0% -> 0%
where the time goes in v1:
time: 1050 us
  waiting for transfers between devices  813 us (77%)
  blocking collectives  104 us (10%)
  matrix products  50 us (5%)
  local copies, waits for them, and re-layouts  42.3 us (4%)
  other arithmetic  21.1 us (2%)
  between operations  14.3 us (1%)
    all_gather x1, waiting for transfers between devices, per_device(): prediction = jnp.sum(lax.all_gather(partial_pred, 'centers'), axis=0)  296 us
    reduce_scatter x1, waiting for transfers between devices, per_device(): lax.psum_scatter(spread, 'centers', scatter_dimension=0, tiled=True)  143 us
    psum x1, waiting for transfers between devices, per_device(): coeff = lax.psum(coeff_part, ('batch', 'centers'))  139 us
    all_gather x1, waiting for transfers between devices, per_device(): lax.all_gather(local_rows, 'centers', axis=0, tiled=True)  131 us
    all_gather x1, blocking collectives, per_device(): all_targets = lax.all_gather(local_targets, 'centers', axis=0, tiled=True)  90.6 us
    psum x1, waiting for transfers between devices, per_device(): correction = lax.psum(corr_part, 'batch')  62.5 us
    psum x1, waiting for transfers between devices, per_device(): grads = lax.psum(grads_part, 'batch')  41.5 us
    dot_general x1, matrix products, kernel_rows(): lax.dot_general(row_block, center_block, (((1,), (1,)), ((), ())), precis...  37 us
  transfers between devices with their start and end apart: 7, of which 6 were waited for; matrix products, arithmetic and copies ran while one was open for 4% of the time, Pallas kernels for 0%

profile of v1, /device:TPU:1, one launch (start us, length us, event | category | flops | bytes accessed | tf_op | source)
XLA Modules:
  0.0 1052.7 jit_solution(9933725225812370396)
XLA Ops:
  7.2 0.0 copy-start
  7.2 0.0 all-gather.6.cloned.1.call-start
  7.2 0.7 compare_select_fusion.4
  7.9 2.2 gather_fusion
  10.2 0.0 all-gather.6.cloned.1.call-update
  10.2 0.0 all-gather.8.cloned.1.call-start
  10.2 1.1 multiply_reduce_fusion.1
  11.4 131.1 %all-gather.6.cloned.1.call-done = f32[2048,128]{1,0:T(8,128)} async-done(((f32[64,128]{1,0:T(8,128)}), f32[2048,128]{1,0:T(8,128)}) %all-gather.6.cloned.1.call-update) | async-done | bytes 1048592 | tf_op jit(solution)/shard_map/all_gather | solution.py:60
  142.5 1.6 multiply_reduce_fusion
  144.1 0.0 copy-start.4
  144.1 37.0 %multiply_add_fusion = f32[2048,512]{1,0:T(8,128)S(1)} fusion(f32[2048,128]{1,0:T(8,128)} %all-gather.6.cloned.1.call-done, f32[512,128]{1,0:T(8,128)} %param.12, f32[512]{0:T(512)S(1)} %multiply_add_fusion.2, f32[2048]{0:T(1024)S(1)} %multiply_add_fusion.1), kind=kOutput, calls=%fused_computation.9 | convolution fusion | flops 1656750080 | bytes 5515264 | tf_op jit(solution)/shard_map/dot_general | solution.py:14
  181.1 0.0 copy-start.1
  181.1 2.0 copy-done.1
  183.1 0.0 copy-done.4
  183.1 5.0 fusion.8
  188.1 0.0 all-gather.8.cloned.1.call-update
  188.1 0.0 copy-done.5
  188.1 0.1 fusion.4
  188.2 0.2 reduce_window_sum.11
  188.4 0.2 select_reduce_fusion
  188.6 0.0 copy-done.7
  188.6 6.4 scatter_fusion
  195.0 0.7 copy.22
  195.7 7.0 all-to-all-start
  202.7 0.0 all-reduce.4.cloned.1.call-start
  202.7 0.0 copy-done.3
  202.8 0.2 copy.20
  203.0 0.6 gather_fusion.1
  203.6 90.6 %all-gather.2 = f32[2048,64]{1,0:T(8,128)S(1)} all-gather(f32[64,64]{1,0:T(8,128)S(1)} %gather_fusion.1), channel_id=4, replica_groups=mesh['batch'=4,'centers'=32] {'centers'}, dimensions={0}, use_global_device_ids=true | all-gather | bytes 540672 | tf_op jit(solution)/shard_map/all_gather | solution.py:63
  294.2 296.1 %all-gather.8.cloned.1.call-done = f32[65536,64]{0,1:T(8,128)} async-done(((f32[2048,64]{0,1:T(8,128)}), f32[65536,64]{0,1:T(8,128)}) %all-gather.8.cloned.1.call-update) | async-done | bytes 16777232 | tf_op jit(solution)/shard_map/all_gather | solution.py:64
  590.3 17.7 %copy.26 = f32[8,8,32,2048]{3,2,1,0:T(8,128)} copy(f32[8,8,32,2048]{3,1,2,0:T(8,128)} %bitcast.36) | data formatting | bytes 33554432
  608.0 8.8 bitcast_reduce_fusion
  616.8 1.3 copy.21
  618.1 1.4 sub.36
  619.5 0.0 copy-start.6
  619.5 5.3 convolution_multiply_fusion
  624.8 0.0 all-reduce.4.cloned.1.call-update
  624.8 0.0 all-reduce.6.cloned.1.call-start
  624.9 0.0 all-to-all-done
  624.9 0.1 reshape.74
  625.0 41.5 %all-reduce.4.cloned.1.call-done = f32[512,64]{0,1:T(8,128)} async-done(((f32[512,64]{0,1:T(8,128)}), f32[512,64]{0,1:T(8,128)}) %all-reduce.4.cloned.1.call-update) | async-done | bytes 131088 | tf_op jit(solution)/shard_map/psum | solution.py:76
  666.5 1.0 copy.23
  667.6 0.7 gather_fusion.2
  668.3 0.1 reshape.109
  668.4 13.8 %all_to_all.17 = f32[32,1,512]{2,1,0:T(1,128)S(1)} all-to-all(f32[32,1,512]{2,1,0:T(1,128)S(1)} %reshape.109), channel_id=1, replica_groups=mesh['batch'=4,'centers'=32] {'centers'}, dimensions={0} | all-to-all | bytes 131072 | tf_op jit(solution)/shard_map/all_to_all | solution.py:86
  682.3 0.5 broadcast.183
  682.8 0.8 reduce
  683.6 0.1 reshape.110
  683.7 1.0 gather_fusion.3
  684.6 1.1 convolution_bitcast_fusion
  685.8 0.0 all-reduce.6.cloned.1.call-update
  685.8 0.3 reduce-scatter.2.cloned.1.call-start
  686.1 139.1 %all-reduce.6.cloned.1.call-done = f32[1024,64]{0,1:T(8,128)} async-done(((f32[1024,64]{0,1:T(8,128)}), f32[1024,64]{0,1:T(8,128)}) %all-reduce.6.cloned.1.call-update) | async-done | bytes 262160 | tf_op jit(solution)/shard_map/psum | solution.py:95
  825.2 1.6 convolution_bitcast_fusion.1
  826.8 0.1 copy.24
  826.9 4.7 scatter_custom_fusion.1
  831.6 6.8 copy.25
  838.4 0.0 reduce-scatter.2.cloned.1.call-update
  838.4 0.0 all-reduce.8.cloned.1.call-start
  838.5 142.6 %reduce-scatter.2.cloned.1.call-done = f32[512,64]{0,1:T(8,128)} async-done(((f32[16384,64]{0,1:T(8,128)}), f32[512,64]{0,1:T(8,128)}) %reduce-scatter.2.cloned.1.call-update) | async-done | bytes 131088 | tf_op jit(solution)/shard_map/reduce_scatter | solution.py:107
  981.1 0.0 all-reduce.8.cloned.1.call-update
  981.1 0.6 constant_dynamic-slice_fusion
  981.7 62.5 %all-reduce.8.cloned.1.call-done = f32[512,64]{0,1:T(8,128)} async-done(((f32[512,64]{0,1:T(8,128)}), f32[512,64]{0,1:T(8,128)}) %all-reduce.8.cloned.1.call-update) | async-done | bytes 131088 | tf_op jit(solution)/shard_map/psum | solution.py:108
  1044.3 1.6 sub.38
  (15 shorter events, 0.1 us)
Async XLA Ops:
  7.2 677.5 %copy-start = (f32[128,1024]{1,0:T(8,128)S(1)}, f32[128,1024]{1,0:T(8,128)}, u32[]{:S(2)}) copy-start(f32[128,1024]{1,0:T(8,128)} %param.14) | copy-start | bytes 1572868
  7.2 135.3 %all-gather.6.cloned.1.call-start = ((), (), s32[]{:S(2)}) async-start(), calls=%async_computation.7 | async-start | bytes 1081344 | tf_op jit(solution)/shard_map/all_gather | solution.py:60
  10.2 580.1 %all-gather.8.cloned.1.call-start = ((), (), s32[]{:S(2)}) async-start(), calls=%async_computation.8 | async-start | bytes 17301504 | tf_op jit(solution)/shard_map/all_gather | solution.py:64
  144.1 39.0 %copy-start.4 = (f32[512,64]{0,1:T(8,128)S(1)}, f32[512,64]{0,1:T(8,128)}, u32[]{:S(2)}) copy-start(f32[512,64]{0,1:T(8,128)} %param.13) | copy-start | bytes 393220
  181.1 2.0 copy-start.1
  183.1 5.0 copy-start.5
  183.1 5.5 copy-start.7
  183.1 19.6 %copy-start.3 = (f32[1024,64]{0,1:T(8,128)S(1)}, f32[1024,64]{0,1:T(8,128)}, u32[]{:S(2)}) copy-start(f32[1024,64]{0,1:T(8,128)} %param.10) | copy-start | bytes 786436
  195.7 429.1 %all-to-all-start = ((s32[32,1,8]{2,1,0:T(1,128)}), s32[32,1,8]{2,1,0:T(1,128)S(1)}, u32[]{:S(2)}, u32[]{:S(2)}) async-start(s32[32,1,8]{2,1,0:T(1,128)} %copy.22), calls=%async_computation | async-start | bytes 32768 | tf_op jit(solution)/shard_map/all_to_all | solution.py:84
  202.7 463.8 %all-reduce.4.cloned.1.call-start = ((), (), s32[]{:S(2)}) async-start(), calls=%async_computation.3 | async-start | bytes 262144 | tf_op jit(solution)/shard_map/psum | solution.py:76
  619.5 205.7 %copy-start.6 = (f32[1024]{0:T(1024)S(1)}, f32[1024]{0:T(1024)}, u32[]{:S(2)}) copy-start(f32[1024]{0:T(1024)} %param.15) | copy-start | bytes 12292
  624.8 200.3 %all-reduce.6.cloned.1.call-start = ((), (), s32[]{:S(2)}) async-start(), calls=%async_computation.4 | async-start | bytes 524288 | tf_op jit(solution)/shard_map/psum | solution.py:95
  685.8 295.3 %reduce-scatter.2.cloned.1.call-start = ((), (), s32[]{:S(2)}) async-start(), calls=%async_computation.5 | async-start | bytes 4325376 | tf_op jit(solution)/shard_map/reduce_scatter | solution.py:107
  838.4 205.9 %copy-start.2 = (f32[512,64]{0,1:T(8,128)S(1)}, f32[512,64]{0,1:T(8,128)}, u32[]{:S(2)}) copy-start(f32[512,64]{0,1:T(8,128)} %all-reduce.4.cloned.1.call-done) | copy-start | bytes 393220
  838.4 205.8 %all-reduce.8.cloned.1.call-start = ((), (), s32[]{:S(2)}) async-start(), calls=%async_computation.6 | async-start | bytes 262144 | tf_op jit(solution)/shard_map/psum | solution.py:108
Sparse Core Ops, SparseCore 0:
  10.3 132.1 all-gather.5
  188.2 402.0 all-gather.7
  624.9 41.5 all-reduce.3
  685.9 139.1 all-reduce.5
  838.6 142.4 reduce-scatter.1
  983.6 60.6 all-reduce.7
